TPU v7x, 128 devices: a whole 4x4x4 slice. The times are simulated.
128 devices in a mesh: row: 8 (over z, core), col: 16 (over y, x).
Axes of the slice: x: 4, y: 4, z: 4, core: 2. Of those that a mesh axis runs over, the one named last changes fastest.
Arguments:
- wrf_forcing: float32 [7, 128, 256], P(None, ('row', 'col')), may hold values from 0 to 1
- ground_height_km: float32 [2048, 4096], P('row', 'col'), may hold values from 0.2 to 3
- reflected_share: float32 [2048, 4096], P('row', 'col'), may hold values from 0.35 to 0.85
- snow_water: float32 [2048, 4096], P('row', 'col'), may hold values from 0 to 6
- soil_water: float32 [2048, 4096], P('row', 'col'), may hold values from 1 to 8
- saturated: float32 [2048, 4096], P('row', 'col'), may hold values from 0.5 to 4
- release_rate: float32 [2048, 4096], P('row', 'col'), may hold values from 0.05 to 0.3
- mfd_weights: bfloat16 [8, 2048, 4096], P(None, 'row', 'col'), may hold values from 0 to 1, as said below
- cell_segment: int32 [2048, 4096], P('row', 'col'), may hold values from 0 to 127
- route_inverse: float32 [128, 2048, 128], P('row', 'col'), may hold values from 0 to 1, as said below
- transfer: float32 [128, 2048], P('row', 'col'), may hold values from 0.96 to 1
- downstream: int32 [128, 16], P('row', 'col'), may hold values from 1 to 16, as said below
Outputs:
- snowpack: float32 [2048, 4096], P('row', 'col')
- soil_moisture: float32 [2048, 4096], P('row', 'col')
- groundwater: float32 [2048, 4096], P('row', 'col')
- channel_flow: float32 [128, 2048], P('row', 'col')
Inputs may be any that keep to these rules, and one draw needn't show every extreme that they name: `mfd_weights`: the eight shares of a cell are positive and add up to less than one. `route_inverse`: entries are positive and every column of each block's 128 by 128 matrix sums to one. `downstream`: block b of a device drains into block b + 1, b + 2 or b + 3 of the same device and column group, and 16 means the flow leaves toward the next column group.
All inputs are finite; a program needn't handle non-finite values.
Results may differ from a plain program's by a relative error of at most 0.0005.
Values may be sent and summed in bfloat16 or wider, within the bound.
A program may use at most 64 MiB of HBM per device.

v0:
```python
import functools

import jax
import jax.numpy as jnp
from jax import lax
from jax.experimental import pallas as pl
from jax.experimental.pallas import tpu as pltpu
from jax.sharding import PartitionSpec as P

MESH = pl.DeviceIdType.MESH
F32, BF16 = jnp.float32, jnp.bfloat16

FAC = 16
VARS = 7
SEG = 128
SWEEPS = 8
NBLK = 16
BR = 16
TILE = 256
RIM = 8
TOP = 16
ROWS = TILE + 32
OFFSETS = ((-1, -1), (-1, 0), (-1, 1), (0, -1), (0, 1), (1, -1), (1, 0), (1, 1))
GROUND, REFLECTED, SNOW, SOIL, STORE, RATE, WEIGHT = range(7)
ARRAYS = 14
MELT = 10.8
SIDE = 4


def split(x):
    high = x.astype(BF16)
    return high, (x - high.astype(F32)).astype(BF16)


def nn(a, b):
    return lax.dot_general(a, b, (((1,), (0,)), ((), ())), preferred_element_type=F32)


def nt(a, b):
    return lax.dot_general(a, b, (((1,), (1,)), ((), ())), preferred_element_type=F32)


def both(x, axis):
    return jnp.concatenate(split(x), axis=axis)


def product(a, b):
    right = both(b, 1)
    wide = nn(both(a, 1), jnp.concatenate([right, right], axis=0))
    return wide[:, :SEG] + wide[:, SEG:]


def product_nt(a, b):
    right = both(b, 0)
    wide = nt(both(a, 1), jnp.concatenate([right, right], axis=1))
    return wide[:, :SEG] + wide[:, SEG:]


def iota(shape, dim):
    return lax.broadcasted_iota(jnp.int32, shape, dim)


def kernel(
    n_row,
    n_col,
    forcing,
    ground,
    reflected,
    snow_water,
    soil_water,
    saturated,
    release,
    mfd,
    segment,
    route,
    transfer,
    downstream,
    snow_out,
    soil_out,
    ground_out,
    flow_out,
    ext,
    wb,
    seg,
    inv,
    wmat,
    fmat,
    mats,
    after,
    tmat,
    gmats,
    ahot,
    bhot,
    hot,
    strips,
    rims,
    wrim,
    mine,
    rows_in,
    spread,
    coarse,
    first_out,
    second_out,
    drained,
    retained,
    trans,
    lat,
    flow0,
    gsend,
    gin,
    load_sem,
    fsend,
    frecv,
    ssend,
    srecv,
    rsend,
    rrecv,
    msend,
    mrecv,
    qsend,
    qrecv,
    gsend_sem,
    grecv,
):
    r, c = lax.axis_index("row"), lax.axis_index("col")
    has_up, has_down = r > 0, r < n_row - 1
    has_left, has_right = c > 0, c < n_col - 1

    barrier = pltpu.get_barrier_semaphore()

    def greet(row, col):
        pl.semaphore_signal(barrier, inc=1, device_id=(row, col), device_id_type=MESH)

    @pl.loop(1, n_col)
    def _(d):
        greet(r, lax.rem(c + d, n_col))

    @pl.when(has_up)
    def _():
        greet(r - 1, c)
        greet(r - 1, n_col - 1)

        @pl.when(has_left)
        def _():
            greet(r - 1, c - 1)

        @pl.when(has_right)
        def _():
            greet(r - 1, c + 1)

    @pl.when(has_down)
    def _():
        greet(r + 1, c)
        greet(r + 1, 0)

        @pl.when(has_left)
        def _():
            greet(r + 1, c - 1)

        @pl.when(has_right)
        def _():
            greet(r + 1, c + 1)

    for k, ref in enumerate((ground, reflected, snow_water, soil_water, saturated, release)):
        for t in range(2):
            pltpu.make_async_copy(
                ref.at[:, pl.ds(128 * t, 128)], ext.at[k, t, pl.ds(TOP, TILE), :], load_sem.at[0]
            ).start()
    load_weights = pltpu.make_async_copy(mfd, wb, load_sem.at[1])
    load_weights.start()
    load_route = pltpu.make_async_copy(route, inv, load_sem.at[2])
    load_route.start()
    for t in range(2):
        pltpu.make_async_copy(
            segment.at[:, pl.ds(128 * t, 128)], seg.at[t], load_sem.at[3]
        ).start()

    eye = (iota((SEG, SEG), 0) == iota((SEG, SEG), 1)).astype(F32)
    wmat[NBLK] = eye
    after[0] = eye
    tmat[0] = eye
    mats[SIDE] = jnp.zeros((SEG, SEG), F32)
    gmats[n_col // SIDE] = jnp.zeros((SEG, SEG), F32)
    gin[c] = jnp.zeros((8, SEG), F32)
    gsend[...] = jnp.zeros((8, SEG), F32)
    fmat[0] = jnp.zeros((SEG, SEG), F32)
    fmat[1] = jnp.zeros((SEG, SEG), F32)
    fmat[2] = eye
    trans[0:3, :] = jnp.ones((3, SEG), F32)
    trans[3 : 3 + NBLK, :] = transfer[...]
    flow0[0:3, :] = jnp.zeros((3, SEG), F32)
    low_half, high_half = c <= n_col // 2, c >= n_col // 2 - 1
    for half in range(2):
        lanes = pl.ds(half * mine.shape[2], mine.shape[2])
        for v in range(VARS):
            mine[half, v : v + 1, :] = forcing[v, :, lanes]
        mine[half, VARS : VARS + 1, :] = jnp.zeros((1, mine.shape[2]), F32)

    @pl.when(jnp.logical_not(low_half))
    def _():
        rows_in[0] = jnp.zeros(rows_in.shape[1:], F32)

    @pl.when(jnp.logical_not(high_half))
    def _():
        rows_in[1] = jnp.zeros(rows_in.shape[1:], F32)

    @pl.when(low_half)
    def _():
        rows_in[0, c + 1] = mine[0]

    @pl.when(high_half)
    def _():
        rows_in[1, c + 1] = mine[1]

    @pl.when(jnp.logical_not(has_up))
    def _():
        ext[:, :, pl.ds(TOP - RIM, RIM), :] = jnp.zeros((ARRAYS, 3, RIM, 128), F32)

    @pl.when(jnp.logical_not(has_down))
    def _():
        ext[:, :, pl.ds(TOP + TILE, RIM), :] = jnp.zeros((ARRAYS, 3, RIM, 128), F32)

    load_weights.wait()
    six = ext.at[pl.ds(0, WEIGHT), pl.ds(0, 2), pl.ds(TOP, TILE), :]
    pltpu.make_async_copy(six, six, load_sem.at[0]).wait()

    step_rows = 64

    def pack_side(side):
        @pl.loop(0, TILE // step_rows)
        def _(i):
            here = pl.ds(pl.multiple_of(i * step_rows, step_rows), step_rows)
            there = pl.ds(pl.multiple_of(TOP + i * step_rows, 8), step_rows)
            lane = iota((step_rows, 128), 1)
            packed = jnp.zeros((step_rows, 128), F32)
            for k in range(ARRAYS):
                if k < WEIGHT:
                    x = ext[k, side, there, :]
                else:
                    x = wb[k - WEIGHT, here, pl.ds(128 * side, 128)].astype(F32)
                shift = (8 * k + 8 * side) % 128
                place = jnp.logical_and(lane >= 8 * k, lane < 8 * k + 8)
                packed = jnp.where(place, pltpu.roll(x, shift, 1) if shift else x, packed)
            strips[side, here, :] = packed

    pack_side(1)

    def strip_copies(side, row_step, row, col):
        source, target, rows = {
            0: (0, RIM, TILE),
            -1: (0, RIM + TILE, RIM),
            1: (TILE - RIM, 0, RIM),
        }[row_step]
        return pltpu.make_async_remote_copy(
            src_ref=strips.at[side, pl.ds(source, rows), :],
            dst_ref=rims.at[side, pl.ds(target, rows), :],
            send_sem=ssend.at[3 * side + row_step + 1],
            recv_sem=srecv.at[3 * side + row_step + 1],
            device_id=(row, col),
            device_id_type=MESH,
        )

    def each_strip(act, sending, sides=(0, 1)):
        for side in sides:
            toward_left = (side == 0) == sending
            there, col = (has_left, c - 1) if toward_left else (has_right, c + 1)
            for row_step in (0, -1, 1):
                ok, row = there, r
                if row_step:
                    toward_up = (row_step == -1) == sending
                    ok = jnp.logical_and(there, has_up if toward_up else has_down)
                    row = r - 1 if toward_up else r + 1

                @pl.when(ok)
                def _():
                    act(strip_copies(side, row_step, row, col))

    pl.semaphore_wait(
        barrier,
        n_col
        - 1
        + (has_up.astype(jnp.int32) + has_down.astype(jnp.int32))
        * (1 + has_left.astype(jnp.int32) + has_right.astype(jnp.int32))
        + jnp.where(jnp.logical_and(c == n_col - 1, has_down), n_col, 0)
        + jnp.where(jnp.logical_and(c == 0, has_up), n_col, 0),
    )

    def forcing_copy(half, row, col, slot, sem):
        return pltpu.make_async_remote_copy(
            src_ref=mine.at[half],
            dst_ref=rows_in.at[half, slot],
            send_sem=fsend.at[2 * sem + half],
            recv_sem=frecv.at[2 * sem + half],
            device_id=(row, col),
            device_id_type=MESH,
        )

    halves = ((0, 0, n_col // 2 + 1), (1, n_col // 2 - 1, n_col))
    sends_down = jnp.logical_and(c == n_col - 1, has_down)
    sends_up = jnp.logical_and(c == 0, has_up)

    @pl.when(sends_down)
    def _():
        for half, start, stop in halves:

            @pl.loop(start, stop)
            def _(d):
                forcing_copy(half, r + 1, d, 0, 1).start()

    @pl.when(sends_up)
    def _():
        for half, start, stop in halves:

            @pl.loop(start, stop)
            def _(d):
                forcing_copy(half, r - 1, d, n_col + 1, 2).start()

    for half, start, stop in halves:

        @pl.loop(start, stop)
        def _(d):
            @pl.when(d != c)
            def _():
                forcing_copy(half, r, d, c + 1, 0).start()

    each_strip(lambda copy: copy.start(), True, (1,))

    def row_copies(side, row):
        source, target = (0, TOP + TILE) if side == 0 else (TILE - RIM, TOP - RIM)

        def remote(src, dst, n):
            return pltpu.make_async_remote_copy(
                src_ref=src,
                dst_ref=dst,
                send_sem=rsend.at[2 * side + n],
                recv_sem=rrecv.at[2 * side + n],
                device_id=(row, c),
                device_id_type=MESH,
            )

        inputs = pl.ds(0, WEIGHT)
        two = pl.ds(0, 2)
        return (
            remote(
                ext.at[inputs, two, pl.ds(TOP + source, RIM), :],
                ext.at[inputs, two, pl.ds(target, RIM), :],
                0,
            ),
            remote(wb.at[:, pl.ds(source, RIM), :], wrim.at[side], 1),
        )

    @pl.when(has_up)
    def _():
        for copy in row_copies(0, r - 1):
            copy.start()

    @pl.when(has_down)
    def _():
        for copy in row_copies(1, r + 1):
            copy.start()

    pack_side(0)
    each_strip(lambda copy: copy.start(), True, (0,))

    load_route.wait()
    pltpu.make_async_copy(seg, seg, load_sem.at[3]).wait()

    def drains_here(block, back):
        before = block - back
        drains = downstream[0, jnp.maximum(before, 0)] == block
        first = jnp.logical_and(block == 0, back == 1)
        return jnp.where(before >= 0, drains, first).astype(F32)

    @pl.loop(0, NBLK)
    def _(i):
        b = NBLK - 1 - i
        later = wmat[downstream[0, b]] * trans[pl.ds(b + 3, 1), :]
        wmat[b] = product(later, inv[b])

        target = pl.ds(pl.multiple_of(i * 16, 16), 16)
        low_part = iota((16, 128), 0)
        for j in range(BR):
            for t in range(2):
                same = jnp.bitwise_and(seg[t, pl.ds(i * BR + j, 1), :], 15) == low_part
                bhot[target, pl.ds(j * TILE + 128 * t, 128)] = jnp.where(same, 1.0, 0.0).astype(
                    BF16
                )

        there = pl.ds(pl.multiple_of(TOP + i * 16, 8), 16)
        for t in range(2):
            kept = None
            for d in range(8):
                x = wb[d, target, pl.ds(128 * t, 128)].astype(F32)
                ext[WEIGHT + d, t, there, :] = x
                kept = x if kept is None else kept + x
            retained[t, there, :] = 1.0 - kept

    across, group = lax.rem(c, SIDE), lax.div(c, SIDE)

    def matrix_copy(to, slot):
        return pltpu.make_async_remote_copy(
            src_ref=wmat.at[0],
            dst_ref=mats.at[slot],
            send_sem=msend.at[to],
            recv_sem=mrecv.at[slot],
            device_id=(r, group * SIDE + to),
            device_id_type=MESH,
        )

    @pl.loop(1, SIDE)
    def _(k):
        matrix_copy(lax.rem(across + k, SIDE), across).start()

    mats[across] = wmat[0]

    cells = 2 * rows_in.shape[3]
    lanes = iota((cells, 384), 1)
    column = jnp.where(lanes < 320, lanes, lanes - 384) + c * TILE
    numerator = 2 * column + 1 - FAC
    point = lax.shift_right_arithmetic(numerator, 5)
    fraction = (numerator - 2 * FAC * point).astype(F32) * (1.0 / (2 * FAC))
    place = iota((cells, 384), 0)
    first = jnp.clip(point, 0, cells - 1)
    second = jnp.clip(point + 1, 0, cells - 1)
    spread[...] = (
        jnp.where(place == first, 1.0 - fraction, 0.0) + jnp.where(place == second, fraction, 0.0)
    ).astype(BF16)

    def many(count, sem, half):
        return pltpu.make_async_remote_copy(
            src_ref=rows_in.at[half, pl.ds(0, count)],
            dst_ref=rows_in.at[half, pl.ds(0, count)],
            send_sem=fsend.at[2 * sem + half],
            recv_sem=frecv.at[2 * sem + half],
            device_id=(r, c),
            device_id_type=MESH,
        )

    for half, needed in ((0, low_half), (1, high_half)):

        @pl.when(needed)
        def _():
            many(n_col - 1, 0, half).wait_recv()

            @pl.when(has_up)
            def _():
                many(1, 1, half).wait_recv()

            @pl.when(has_down)
            def _():
                many(1, 2, half).wait_recv()

            @pl.when(jnp.logical_not(has_up))
            def _():
                rows_in[half, 0] = rows_in[half, 1]

            @pl.when(jnp.logical_not(has_down))
            def _():
                rows_in[half, n_col + 1] = rows_in[half, n_col]

    points = jnp.concatenate(
        [rows_in[half].reshape((n_col + 2) * 8, cells // 2) for half in range(2)], axis=1
    )
    high, rest = split(points)
    middle, low = split(points - high.astype(F32))
    weights = spread[...]
    wide = nn(high, weights) + (nn(middle, weights) + nn(low, weights))
    var = jnp.bitwise_and(iota((wide.shape[0], 128), 0), 7)
    scale, shift = jnp.zeros(var.shape, F32), jnp.zeros(var.shape, F32)
    for v, (slope, start) in enumerate(
        (
            (20.0, -10.0 + 6.5 * 0.5),
            (0.8 * MELT, 0.0),
            (0.15 * MELT, (0.25 - 0.3) * MELT),
            (0.2 * 1.5, 0.0),
            (6.0, 0.5),
            (4.0, 0.0),
        )
    ):
        scale = jnp.where(var == v, slope, scale)
        shift = jnp.where(var == v, start, shift)
    for t in range(3):
        part = wide[:, 128 * t : 128 * t + 128]
        height = pltpu.roll(part, part.shape[0] - 6, 0)
        part = part * scale + shift + jnp.where(var == 0, 13.0 * height, 0.0)
        coarse[0, t] = part
        coarse[1, t, 0 : (n_col + 1) * 8, :] = part[8:] - part[:-8]

    @pl.when(has_up)
    def _():
        for copy in row_copies(1, r - 1):
            copy.wait_recv()
        for copy in row_copies(0, r - 1):
            copy.wait_send()
        for t in range(2):
            for d in range(8):
                ext[WEIGHT + d, t, pl.ds(TOP - RIM, RIM), :] = wrim[
                    1, d, :, pl.ds(128 * t, 128)
                ].astype(F32)

    @pl.when(has_down)
    def _():
        for copy in row_copies(0, r + 1):
            copy.wait_recv()
        for copy in row_copies(1, r + 1):
            copy.wait_send()
        for t in range(2):
            for d in range(8):
                ext[WEIGHT + d, t, pl.ds(TOP + TILE, RIM), :] = wrim[
                    0, d, :, pl.ds(128 * t, 128)
                ].astype(F32)

    for out in (first_out, second_out):
        out[:, 0 : TOP - RIM, :] = jnp.zeros((3, TOP - RIM, 128), F32)
        out[:, TOP + TILE + RIM :, :] = jnp.zeros((3, RIM, 128), F32)

    def balance(k, t):
        rows = pl.ds(pl.multiple_of(TOP - RIM + FAC * k, 8), FAC)
        part = (2 * iota((FAC, 128), 0) + 1).astype(F32) * (1.0 / (2 * FAC))
        v = []
        for var in range(6):
            at = pl.ds(k * 8 + var, 1)
            v.append(coarse[0, t, at, :] + coarse[1, t, at, :] * part)
        heat, solar, thermal, deficit, breeze, rain = v
        heat = heat - 6.5 * ext[GROUND, t, rows, :]
        frozen = rain / (1.0 + jnp.exp(heat * (1.0 / 1.5)))
        liquid = rain - frozen
        budget = (solar - solar * ext[REFLECTED, t, rows, :]) + thermal
        budget = budget + (0.02 * MELT) * breeze * heat
        pack = ext[SNOW, t, rows, :] + frozen
        melted = jnp.minimum(jnp.maximum(budget, 0.0), pack)
        wetted = ext[SOIL, t, rows, :] + liquid + melted
        demand = (0.3 / MELT) * solar + (deficit + (0.1 * deficit) * breeze)
        evaporation = demand * wetted / (wetted + 2.0)
        remaining = wetted - evaporation
        recharge = 0.4 * jnp.maximum(remaining - 6.0, 0.0)
        storage = ext[STORE, t, rows, :] + recharge
        ext[STORE, t, rows, :] = storage
        first_out[t, rows, :] = ext[RATE, t, rows, :] * storage
        if t < 2:
            snow_out[t, rows, :] = pack - melted
            soil_out[t, rows, :] = remaining - recharge
            drained[t, rows, :] = jnp.zeros((FAC, 128), F32)

    balance(0, 0)
    balance(0, 1)

    @pl.loop(0, TILE // FAC // 2)
    def _(i):
        for k in range(2):
            for t in range(2):
                balance(2 * i + 1 + k, t)

    each_strip(lambda copy: copy.wait_recv(), False)

    def unpack(source, target, rows, right_ok, left_ok):
        lane = iota((rows, 128), 1)
        kept = jnp.logical_or(
            jnp.logical_and(lane < RIM, right_ok), jnp.logical_and(lane >= 128 - RIM, left_ok)
        )
        from_right = rims[0, source, :]
        from_left = pltpu.roll(rims[1, source, :], 128 - 8, 1)
        first_half = jnp.bitwise_and(lane, 15) < 8
        pairs = (
            jnp.where(first_half, from_right, from_left),
            jnp.where(first_half, from_left, from_right),
        )
        for k in range(ARRAYS):
            x = pairs[k % 2]
            x = pltpu.roll(x, 128 - 8 * k, 1) if k else x
            ext[k, 2, target, :] = jnp.where(kept, x, 0.0)

    @pl.loop(0, TILE // step_rows)
    def _(i):
        unpack(
            pl.ds(pl.multiple_of(RIM + i * step_rows, 8), step_rows),
            pl.ds(pl.multiple_of(TOP + i * step_rows, 8), step_rows),
            step_rows,
            has_right,
            has_left,
        )

    for source, ok in ((0, has_up), (RIM + TILE, has_down)):
        unpack(
            pl.ds(source, RIM),
            pl.ds(TOP - RIM + source, RIM),
            RIM,
            jnp.logical_and(has_right, ok),
            jnp.logical_and(has_left, ok),
        )

    balance(0, 2)

    @pl.loop(0, TILE // FAC // 4)
    def _(i):
        for k in range(4):
            balance(4 * i + 1 + k, 2)

    def sweep(now, later):
        for q in range((TILE + 2 * RIM) // 16):
            base = TOP - RIM + 16 * q
            rows = pl.ds(base, 16)
            lane = iota((16, 128), 1)
            sums = {-1: [], 0: [], 1: []}
            middle = []
            for t in range(3):
                parts = {-1: None, 0: None, 1: None}
                for down_row in (-1, 0, 1):
                    at = pl.ds(base - down_row, 16)
                    out = now[t, at, :]
                    if down_row == 0:
                        middle.append(out)
                    for direction, (dr, dc) in enumerate(OFFSETS):
                        if dr == down_row:
                            term = ext[WEIGHT + direction, t, at, :] * out
                            parts[dc] = term if parts[dc] is None else parts[dc] + term
                for dc in (-1, 0, 1):
                    sums[dc].append(parts[dc])
            east = [pltpu.roll(x, 1, 1) for x in sums[1]]
            west = [pltpu.roll(x, 127, 1) for x in sums[-1]]
            for t in range(3):
                inflow = (
                    sums[0][t]
                    + jnp.where(lane == 0, east[(t + 2) % 3], east[t])
                    + jnp.where(lane == 127, west[(t + 1) % 3], west[t])
                )
                storage = (ext[STORE, t, rows, :] - middle[t]) + inflow
                ext[STORE, t, rows, :] = storage
                later[t, rows, :] = ext[RATE, t, rows, :] * storage
                if t < 2:
                    drained[t, rows, :] = drained[t, rows, :] + middle[t]

    @pl.loop(0, SWEEPS // 2)
    def _(i):
        @pl.when(i == 1)
        def _():
            @pl.loop(1, SIDE)
            def _(k):
                slot = lax.rem(across + k, SIDE)
                matrix_copy(slot, slot).wait_recv()

            after[1] = mats[SIDE - 1]
            tmat[1] = mats[jnp.where(across > 0, across - 1, SIDE)]

        after[i + 1] = product(after[i], mats[jnp.where(i > 0, SIDE - 1 - i, SIDE)])
        started = jnp.logical_and(i > 0, i < across)
        tmat[i + 1] = product(tmat[i], mats[jnp.where(started, across - 1 - i, SIDE)])
        sweep(first_out, second_out)
        sweep(second_out, first_out)

    def group_copy(to, slot):
        return pltpu.make_async_remote_copy(
            src_ref=after.at[SIDE],
            dst_ref=gmats.at[slot],
            send_sem=qsend.at[to],
            recv_sem=qrecv.at[slot],
            device_id=(r, to * SIDE + across),
            device_id_type=MESH,
        )

    @pl.loop(group + 1, n_col // SIDE)
    def _(later):
        group_copy(later, group).start()

    for t in range(2):
        own = pl.ds(TOP, TILE)
        ground_out[t, own, :] = ext[STORE, t, own, :]
        drained[t, own, :] = drained[t, own, :] * retained[t, own, :]

    def build(piece):
        top = iota((8, 128), 0)
        for b in range(NBLK):
            for i in range(4 * piece, 4 * piece + 4):
                for t in range(2):
                    lanes = pl.ds(TILE * i + 128 * t, 128)
                    row = b * BR + i
                    same = lax.shift_right_logical(seg[t, row : row + 1, :], 4) == top
                    kept = jnp.where(same, drained[t, TOP + row : TOP + row + 1, :], 0.0)
                    high, low = split(kept)
                    ahot[16 * b : 16 * b + 8, lanes] = high
                    ahot[16 * b + 8 : 16 * b + 16, lanes] = low

    build(0)
    for i in range(4):
        if i < 3:
            build(i + 1)
        wide = pl.ds(4 * TILE * i, 4 * TILE)
        piece = nt(ahot[:, wide], bhot[:, wide])
        for t in range(2):
            half = piece[:, 128 * t : 128 * t + 128]
            hot[t] = half if i == 0 else hot[t] + half

    lane = iota((8, 128), 1)
    sixteen = lax.shift_right_logical(lane, 4)
    for b in range(NBLK):
        t = b // 8
        x = hot[t, b * 16 : b * 16 + 8, :] + hot[t, b * 16 + 8 : b * 16 + 16, :]
        x = jnp.where(sixteen == b % 8, x, 0.0)
        for shift in (16, 32, 64):
            x = x + pltpu.roll(x, shift, 1)
        x = jnp.where(sixteen == iota((8, 128), 0), x, 0.0)
        lat[b : b + 1, :] = 0.001 * jnp.sum(x, axis=0, keepdims=True)

    def to_row(matrix):
        column = jnp.sum(matrix, axis=1, keepdims=True)
        same = iota((SEG, SEG), 0) == iota((SEG, SEG), 1)
        return jnp.sum(jnp.where(same, column, 0.0), axis=0, keepdims=True)

    total = wmat[0] * lat[0:1, :]
    for b in range(1, NBLK):
        total = total + wmat[b] * lat[b : b + 1, :]
    leaving = to_row(total)
    gsend[0:1, :] = leaving
    gsend[1:2, :] = to_row(after[SIDE - 1 - across] * leaving)

    def leaving_copy(col, slot):
        return pltpu.make_async_remote_copy(
            src_ref=gsend,
            dst_ref=gin.at[slot],
            send_sem=gsend_sem.at[col],
            recv_sem=grecv.at[slot],
            device_id=(r, col),
            device_id_type=MESH,
        )

    @pl.loop(c + 1, n_col)
    def _(col):
        leaving_copy(col, c).start()

    @pl.loop(0, NBLK)
    def _(b):
        source = lat[pl.ds(b, 1), :]
        carried = jnp.zeros((SEG, SEG), F32)
        for back in range(1, 4):
            share = trans[pl.ds(b + 3 - back, 1), :] * drains_here(b, back)
            carried = carried + fmat[b + 3 - back] * share
            source = source + share * flow0[pl.ds(b + 3 - back, 1), :]
        fmat[b + 3] = product_nt(carried, inv[b])
        flow0[pl.ds(b + 3, 1), :] = to_row(inv[b] * source)

    @pl.loop(0, group)
    def _(slot):
        group_copy(group, slot).wait_recv()

    reach = [tmat[across]]
    for j in range(n_col // SIDE - 2):
        slot = jnp.where(j < group, group - 1 - j, n_col // SIDE)
        reach.append(product(reach[j], gmats[slot]))

    @pl.loop(0, c)
    def _(slot):
        leaving_copy(c, slot).wait_recv()

    total = jnp.zeros((SEG, SEG), F32)
    for j in range(n_col // SIDE - 1):
        arriving = jnp.zeros((1, SEG), F32)
        for k in range(SIDE):
            slot = jnp.where(j < group, (group - 1 - j) * SIDE + k, c)
            arriving = arriving + gin[slot, 1:2, :]
        total = total + reach[j] * arriving
    for k in range(SIDE - 1):
        slot = jnp.where(k < across, c - 1 - k, c)
        total = total + tmat[k] * gin[slot, 0:1, :]
    entering = jnp.sum(total, axis=1, keepdims=True)

    for b in range(NBLK):
        extra = jnp.sum(fmat[b + 3] * entering, axis=0, keepdims=True)
        flow_out[b : b + 1, :] = flow0[b + 3 : b + 4, :] + extra

    for half, needed in ((0, low_half), (1, high_half)):

        @pl.when(needed)
        def _():
            many(n_col // 2, 0, half).wait_send()

        @pl.when(jnp.logical_not(needed))
        def _():
            many(n_col // 2 + 1, 0, half).wait_send()

        for sem, sends in ((1, sends_down), (2, sends_up)):

            @pl.when(sends)
            def _():
                many(n_col // 2 + 1, sem, half).wait_send()

    @pl.loop(1, SIDE)
    def _(k):
        matrix_copy(lax.rem(across + k, SIDE), across).wait_send()

    @pl.loop(group + 1, n_col // SIDE)
    def _(later):
        group_copy(later, group).wait_send()

    each_strip(lambda copy: copy.wait_send(), True)

    @pl.loop(c + 1, n_col)
    def _(col):
        leaving_copy(col, c).wait_send()


def writer(*refs):
    snow, soil, water, flow, snow_out, soil_out, ground_out, flow_out, sems = refs
    copies = [pltpu.make_async_copy(flow, flow_out, sems.at[6])]
    for k, (ref, out) in enumerate(((snow, snow_out), (soil, soil_out), (water, ground_out))):
        for t in range(2):
            copies.append(
                pltpu.make_async_copy(
                    ref.at[t, pl.ds(TOP, TILE), :],
                    out.at[:, pl.ds(128 * t, 128)],
                    sems.at[2 * k + t],
                )
            )
    for copy in copies:
        copy.start()
    for copy in copies:
        copy.wait()


def per_device(n_row, n_col, forcing, *args):
    *args, downstream = args
    cells = forcing.shape[2]
    any_space = pl.BlockSpec(memory_space=pl.ANY)
    vmem = pl.BlockSpec(memory_space=pltpu.VMEM)
    smem = pl.BlockSpec(memory_space=pltpu.SMEM)
    tile = jax.ShapeDtypeStruct((TILE, TILE), F32)
    flows = jax.ShapeDtypeStruct((NBLK, SEG), F32)
    dma = pltpu.SemaphoreType.DMA
    results = pl.pallas_call(
        functools.partial(kernel, n_row, n_col),
        out_shape=(*(pltpu.VMEM((2, ROWS, 128), F32) for _ in range(3)), pltpu.VMEM((NBLK, SEG), F32)),
        in_specs=[vmem] + [any_space] * 9 + [vmem, smem],
        out_specs=(vmem, vmem, vmem, vmem),
        scratch_shapes=[
            pltpu.VMEM((ARRAYS, 3, ROWS, 128), F32),
            pltpu.VMEM((8, TILE, TILE), BF16),
            pltpu.VMEM((2, TILE, 128), jnp.int32),
            pltpu.VMEM((NBLK, SEG, SEG), F32),
            pltpu.VMEM((NBLK + 1, SEG, SEG), F32),
            pltpu.VMEM((NBLK + 3, SEG, SEG), F32),
            pltpu.VMEM((SIDE + 1, SEG, SEG), F32),
            pltpu.VMEM((SIDE + 1, SEG, SEG), F32),
            pltpu.VMEM((SIDE + 1, SEG, SEG), F32),
            pltpu.VMEM((n_col // SIDE + 1, SEG, SEG), F32),
            pltpu.VMEM((TILE, BR * TILE), BF16),
            pltpu.VMEM((TILE, BR * TILE), BF16),
            pltpu.VMEM((2, TILE, 128), F32),
            pltpu.VMEM((2, TILE, 128), F32),
            pltpu.VMEM((2, TILE + 2 * RIM, 128), F32),
            pltpu.VMEM((2, 8, RIM, TILE), BF16),
            pltpu.VMEM((2, 8, cells // 2), F32),
            pltpu.VMEM((2, n_col + 2, 8, cells // 2), F32),
            pltpu.VMEM((cells, 384), BF16),
            pltpu.VMEM((2, 3, (n_col + 2) * 8, 128), F32),
            pltpu.VMEM((3, ROWS, 128), F32),
            pltpu.VMEM((3, ROWS, 128), F32),
            pltpu.VMEM((2, ROWS, 128), F32),
            pltpu.VMEM((2, ROWS, 128), F32),
            pltpu.VMEM((24, SEG), F32),
            pltpu.VMEM((NBLK, SEG), F32),
            pltpu.VMEM((24, SEG), F32),
            pltpu.VMEM((8, SEG), F32),
            pltpu.VMEM((n_col, 8, SEG), F32),
            dma((4,)),
            dma((6,)),
            dma((6,)),
            dma((6,)),
            dma((6,)),
            dma((4,)),
            dma((4,)),
            dma((SIDE,)),
            dma((SIDE,)),
            dma((n_col // SIDE,)),
            dma((n_col // SIDE,)),
            dma((n_col,)),
            dma((n_col,)),
        ],
        compiler_params=pltpu.CompilerParams(
            collective_id=0, has_side_effects=True
        ),
        name="hydrology",
    )(forcing, *args, downstream.T)
    return pl.pallas_call(
        writer,
        out_shape=(tile, tile, tile, flows),
        in_specs=[any_space] * 4,
        out_specs=(any_space,) * 4,
        scratch_shapes=[dma((7,))],
        compiler_params=pltpu.CompilerParams(vmem_limit_bytes=1 << 20),
        name="writer",
    )(*results)


def solution(mesh):
    n_row, n_col = mesh.shape["row"], mesh.shape["col"]
    tiles = P("row", "col")
    placed = (
        P(None, ("row", "col"), None),
        *(tiles for _ in range(6)),
        P(None, "row", "col"),
        tiles,
        P("row", "col", None),
        tiles,
        tiles,
    )
    return jax.shard_map(
        functools.partial(per_device, n_row, n_col),
        mesh=mesh,
        in_specs=placed,
        out_specs=(tiles, tiles, tiles, tiles),
        check_vma=False,
    )
```

profile of v0, /device:TPU:9, one launch (start us, length us, event | category | flops | bytes accessed | tf_op | source)
XLA Modules:
  0.0 26.9 jit_solution(3953566623175830665)
XLA Ops:
  0.6 25.4 %hydrology.1 = (f32[2,288,128]{2,1,0:T(8,128)S(1)}, f32[2,288,128]{2,1,0:T(8,128)S(1)}, f32[2,288,128]{2,1,0:T(8,128)S(1)}, f32[16,128]{1,0:T(8,128)S(1)}) custom-call(f32[7,1,256]{2,1,0:T(1,128)} %forcing.1, f32[256,256]{1,0:T(8,128)} %ground.1, f32[256,256]{1,0:T(8,128)} %reflected.1, f32[256,256]{1,0:T(8,128)} %snow_water.1, f32[256,256]{1,0:T(8,128)} %soil_water.1, ...), custom_call_target="tpu_custom_call" | custom-call | tf_op jit(solution)/shard_map/hydrology/pallas_call | solution.py:828
  26.0 0.9 %writer.1 = (f32[256,256]{1,0:T(8,128)}, f32[256,256]{1,0:T(8,128)}, f32[256,256]{1,0:T(8,128)}, f32[16,128]{1,0:T(8,128)}) custom-call(f32[2,288,128]{2,1,0:T(8,128)S(1)} %get-tuple-element.8.refs_0_, f32[2,288,128]{2,1,0:T(8,128)S(1)} %get-tuple-element.9.refs_1_, f32[2,288,128]{2,1,0:T(8,128)S(1)} %get-tuple-element.10.refs_2_, ...), custom_call_target="tpu_custom_call" | custom-call | tf_op jit(solution)/shard_map/writer/pallas_call | solution.py:882
where the time goes:
time: 27.1 us; the launch traced here: 26.9 us
  Pallas kernels  26.3 us (97%)
  between operations  0.64 us (2%)
    pallas_call x1, Pallas kernels, per_device(): pl.pallas_call(functools.partial(kernel, n_row, n_col), out_shape=(*(pltp...  25.4 us
    pallas_call x1, Pallas kernels, per_device(): pl.pallas_call(writer, out_shape=(tile, tile, tile, flows), in_specs=[any...  0.94 us

commit v1 on v0

--- a/solution.py
+++ b/solution.py
@@ -131,8 +131,7 @@
     def greet(row, col):
         pl.semaphore_signal(barrier, inc=1, device_id=(row, col), device_id_type=MESH)
 
-    @pl.loop(1, n_col)
-    def _(d):
+    for d in range(1, n_col):
         greet(r, lax.rem(c + d, n_col))
 
     @pl.when(has_up)
@@ -244,6 +243,7 @@
             strips[side, here, :] = packed
 
     pack_side(1)
+    pack_side(0)
 
     def strip_copies(side, row_step, row, col):
         source, target, rows = {
@@ -359,7 +359,6 @@
         for copy in row_copies(1, r + 1):
             copy.start()
 
-    pack_side(0)
     each_strip(lambda copy: copy.start(), True, (0,))
 
     load_route.wait()

time: 27.1 us -> 26.9 us (level)
  the two profiles are of different devices: /device:TPU:9 before, /device:TPU:40 now
where the time goes in v1:
time: 26.9 us; the launch traced here: 26.4 us
  Pallas kernels  25.7 us (96%)
  between operations  0.64 us (2%)
    pallas_call x1, Pallas kernels, per_device(): pl.pallas_call(functools.partial(kernel, n_row, n_col), out_shape=(*(pltp...  24.8 us
    pallas_call x1, Pallas kernels, per_device(): pl.pallas_call(writer, out_shape=(tile, tile, tile, flows), in_specs=[any...  0.94 us

profile of v1, /device:TPU:40, one launch (start us, length us, event | category | flops | bytes accessed | tf_op | source)
XLA Modules:
  0.0 26.4 jit_solution(2037753227173130280)
XLA Ops:
  0.6 24.8 %hydrology.1 = (f32[2,288,128]{2,1,0:T(8,128)S(1)}, f32[2,288,128]{2,1,0:T(8,128)S(1)}, f32[2,288,128]{2,1,0:T(8,128)S(1)}, f32[16,128]{1,0:T(8,128)S(1)}) custom-call(f32[7,1,256]{2,1,0:T(1,128)} %forcing.1, f32[256,256]{1,0:T(8,128)} %ground.1, f32[256,256]{1,0:T(8,128)} %reflected.1, f32[256,256]{1,0:T(8,128)} %snow_water.1, f32[256,256]{1,0:T(8,128)} %soil_water.1, ...), custom_call_target="tpu_custom_call" | custom-call | tf_op jit(solution)/shard_map/hydrology/pallas_call | solution.py:827
  25.4 0.9 %writer.1 = (f32[256,256]{1,0:T(8,128)}, f32[256,256]{1,0:T(8,128)}, f32[256,256]{1,0:T(8,128)}, f32[16,128]{1,0:T(8,128)}) custom-call(f32[2,288,128]{2,1,0:T(8,128)S(1)} %get-tuple-element.8.refs_0_, f32[2,288,128]{2,1,0:T(8,128)S(1)} %get-tuple-element.9.refs_1_, f32[2,288,128]{2,1,0:T(8,128)S(1)} %get-tuple-element.10.refs_2_, ...), custom_call_target="tpu_custom_call" | custom-call | tf_op jit(solution)/shard_map/writer/pallas_call | solution.py:881
